TPU v7x, 32 devices: a whole 2x2x4 slice. The times are simulated.
32 devices in a mesh: req: 8 (over z, y), tp: 4 (over x, core).
Axes of the slice: x: 2, y: 2, z: 4, core: 2. Of those that a mesh axis runs over, the one named last changes fastest.
Arguments:
- tokens: bfloat16 [16, 256, 2048], P('req'), may hold values from -6 to 6
- attn_gain: float32 [2048], replicated, may hold values from 0.25 to 1.75
- w_query: bfloat16 [2048, 1280], P(None, 'tp'), may hold values from -0.125 to 0.125
- key_value_weight: bfloat16 [2048, 640], replicated, may hold values from -0.125 to 0.125
- w_out: bfloat16 [1280, 2048], P('tp'), may hold values from -0.15625 to 0.15625
- q_gain: float32 [64], replicated, as said below
- k_gain: float32 [64], replicated, as said below
- stored: bfloat16 [8, 5, 2048, 128], P('req'), may hold values from -6 to 6
- continuing: int32 [16], replicated, may hold values from 0 to 1, as said below
- cache_row: int32 [16], replicated, may hold values from -1 to 7, as said below
- cache_len: int32 [16], replicated, may hold values from 0 to 2048, as said below
Outputs:
- layer: bfloat16 [16, 256, 2048], P('req')
- decoding_group_cache: bfloat16 [32, 5, 1152, 128], P('req', None, 'tp')
Inputs may be any that keep to these rules, and one draw needn't show every extreme that they name: `continuing`: exactly 8 requests have 1. `cache_row`: a continuing request's row of stored; every row belongs to exactly one continuing request; -1 for the others. `cache_len`: 1 to 2048 for a continuing request, 2048 for at least one; 0 for the others. `q_gain`: positive. `k_gain`: positive.
All inputs are finite; a program needn't handle non-finite values.
Results may differ from a plain program's by a relative error of at most 0.005.
The roundings to bfloat16 on the way count: a program that leaves them out, or rounds other values in their place, can miss the bound.
Values may be sent and summed in bfloat16 or wider, within the bound.
No kernel may reach another device: no remote copies, remote signals or barrier semaphores. Data moves between devices by JAX's collectives and lax.ppermute only.
A program may use at most 128 MiB of HBM per device.

v0:
```python
import math
import jax
import jax.numpy as jnp
from jax import lax
from jax.sharding import PartitionSpec as P


def swapped(value, axis, apart):
    mask = 2**apart
    pairs = [(source, source ^ mask) for source in range(lax.axis_size(axis))]
    return lax.ppermute(value, axis, pairs)


def normalize(values, gain):
    return values * lax.rsqrt(jnp.mean(values * values, axis=-1, keepdims=True) + 1e-06) * gain


def rotary(values, positions):
    half_dim = values.shape[-1] // 2
    freq = jnp.exp(
        -math.log(10000.0) * jnp.arange(half_dim).astype(jnp.float32) * 2.0 / values.shape[-1]
    )
    angle = positions.astype(jnp.float32)[..., None] * freq
    cosine = jnp.cos(angle)[..., None, :]
    sine = jnp.sin(angle)[..., None, :]
    first_half = values[..., :half_dim]
    second_half = values[..., half_dim:]
    return jnp.concatenate(
        [first_half * cosine - second_half * sine, second_half * cosine + first_half * sine],
        axis=-1,
    )


def attend(query_one, keys_one, allowed, head_dim, new_count, scale):
    scores = (
        jnp.einsum(
            "hqd,hkd->hqk", query_one, keys_one[..., :head_dim], preferred_element_type=jnp.float32
        )
        * scale
    )
    scores = jnp.where(allowed[None], scores, -jnp.inf)
    row_max = jnp.max(scores, axis=-1, keepdims=True)
    weights = jnp.exp(scores - row_max)
    probs = (weights / jnp.sum(weights, axis=-1, keepdims=True)).astype(jnp.bfloat16)
    mixed = jnp.einsum(
        "hqk,hkd->qhd", probs, keys_one[..., head_dim:], preferred_element_type=jnp.float32
    )
    return mixed.astype(jnp.bfloat16).reshape(new_count, query_one.shape[0] * head_dim)


def on_device(
    tokens,
    attn_gain,
    w_query,
    key_value_weight,
    w_out,
    q_gain,
    k_gain,
    stored,
    continuing,
    cache_row,
    cache_len,
):
    tp_count = lax.axis_size("tp")
    req_place = lax.axis_index("req")
    tp_place = lax.axis_index("tp")
    req_dev, new_count, width = tokens.shape
    head_dim = q_gain.shape[0]
    kv_heads = key_value_weight.shape[1] // (2 * head_dim)
    local_heads = w_query.shape[1] // head_dim
    query_group_ratio = local_heads * tp_count // kv_heads
    cache_span = stored.shape[2]
    total_length = cache_span + new_count
    scale = 1.0 / math.sqrt(head_dim)
    relayed = lax.all_to_all(stored, "req", split_axis=2, concat_axis=0, tiled=True)
    live_all = continuing == 1
    rows_all = jnp.where(live_all, cache_row, 0)
    select_chosen = jnp.take(relayed, rows_all, axis=0)
    stored_entries = lax.all_to_all(
        jnp.where(live_all[:, None, None, None], select_chosen, jnp.zeros_like(select_chosen)),
        "req",
        split_axis=0,
        concat_axis=2,
        tiled=True,
    )
    first = req_place * req_dev
    my_live = lax.dynamic_slice_in_dim(continuing, first, req_dev) == 1
    my_len = jnp.where(my_live, lax.dynamic_slice_in_dim(cache_len, first, req_dev), 0)
    position = jnp.arange(cache_span, dtype=jnp.int32)
    stored_entries = jnp.where(
        (position[None, :] < my_len[:, None])[:, None, :, None],
        stored_entries,
        jnp.zeros_like(stored_entries),
    )
    token_rows = tokens.reshape(req_dev * new_count, width)
    normalized_input = normalize(token_rows.astype(jnp.float32), attn_gain).astype(jnp.bfloat16)
    positions = my_len[:, None] + jnp.arange(new_count, dtype=jnp.int32)[None, :]
    query = jnp.dot(normalized_input, w_query, preferred_element_type=jnp.float32).reshape(
        req_dev, new_count, local_heads, head_dim
    )
    query = rotary(normalize(query, q_gain), positions).astype(jnp.bfloat16)
    key_value_rows = jnp.dot(
        normalized_input, key_value_weight, preferred_element_type=jnp.float32
    ).reshape(req_dev, new_count, kv_heads, 2 * head_dim)
    keys_new = rotary(normalize(key_value_rows[..., :head_dim], k_gain), positions)
    fresh = jnp.concatenate([keys_new, key_value_rows[..., head_dim:]], axis=-1).astype(
        jnp.bfloat16
    )
    fresh = jnp.transpose(fresh, (0, 2, 1, 3))
    keys_all = jnp.concatenate([stored_entries, fresh], axis=2)
    head_select = (
        tp_place * local_heads + jnp.arange(local_heads, dtype=jnp.int32)
    ) // query_group_ratio
    query_index = jnp.arange(new_count, dtype=jnp.int32)[:, None]
    key_index = jnp.arange(total_length, dtype=jnp.int32)[None, :]
    outputs = []
    for number in range(req_dev):
        query_one = jnp.transpose(query[number], (1, 0, 2))
        chosen = jnp.take(keys_all[number], head_select, axis=0)
        allowed = jnp.where(
            key_index < cache_span,
            key_index < my_len[number],
            key_index - cache_span <= query_index,
        )
        mixed = attend(query_one, chosen, allowed, head_dim, new_count, scale)
        outputs.append(mixed)
    mixed_all = jnp.concatenate(outputs, axis=0)
    summed = lax.psum(jnp.dot(mixed_all, w_out, preferred_element_type=jnp.float32), "tp")
    layer = (token_rows.astype(jnp.float32) + summed).astype(jnp.bfloat16)
    layer = layer.reshape(req_dev, new_count, width)
    padded_tokens = jnp.concatenate(
        [stored_entries, jnp.zeros((req_dev, kv_heads, new_count, 2 * head_dim), jnp.bfloat16)],
        axis=2,
    )
    whole = jax.vmap(
        lambda padded_one, fresh_one, offset: lax.dynamic_update_slice_in_dim(
            padded_one, fresh_one, offset, 1
        )
    )(padded_tokens, fresh, my_len)
    half_span = total_length // 2
    segment = half_span // tp_count
    pair_side = req_place % 2
    kept_half = lax.dynamic_slice_in_dim(
        whole, pair_side * half_span + tp_place * segment, segment, 2
    )
    sent_half = lax.dynamic_slice_in_dim(
        whole, (1 - pair_side) * half_span + tp_place * segment, segment, 2
    )
    partner = swapped(sent_half, "req", 0)
    decoding_group_cache = jnp.where(
        pair_side == 0,
        jnp.concatenate([kept_half, partner], axis=0),
        jnp.concatenate([partner, kept_half], axis=0),
    )
    return (layer, decoding_group_cache)


def solution(mesh):
    return jax.shard_map(
        on_device,
        mesh=mesh,
        in_specs=(
            P("req", None, None),
            P(),
            P(None, "tp"),
            P(),
            P("tp", None),
            P(),
            P(),
            P("req", None, None, None),
            P(),
            P(),
            P(),
        ),
        out_specs=(P("req", None, None), P("req", None, "tp", None)),
        check_vma=False,
    )
```

profile of v0, /device:TPU:0, one launch (start us, length us, event | category | flops | bytes accessed | tf_op | source)
XLA Modules:
  0.0 405.0 jit_solution(1439324511392412007)
XLA Ops:
  7.2 5.2 %copy.40 = bf16[1,5,2048,128]{3,1,0,2:T(8,128)(2,1)} copy(bf16[1,5,2048,128]{3,2,1,0:T(8,128)(2,1)} %param.20) | data formatting | bytes 5242880 | tf_op args[7]
  12.4 7.4 %all-to-all-start = ((bf16[1,5,2048,128]{3,1,0,2:T(8,128)(2,1)}), bf16[1,5,2048,128]{3,1,0,2:T(8,128)(2,1)}, u32[]{:S(2)}, u32[]{:S(2)}) async-start(bf16[1,5,2048,128]{3,1,0,2:T(8,128)(2,1)} %copy.40), calls=%async_computation | async-start | bytes 8388608 | tf_op jit(solution)/shard_map/all_to_all | solution.py:75
  19.9 93.2 %all-to-all-done = bf16[1,5,2048,128]{3,1,0,2:T(8,128)(2,1)} async-done(((bf16[1,5,2048,128]{3,1,0,2:T(8,128)(2,1)}), bf16[1,5,2048,128]{3,1,0,2:T(8,128)(2,1)}, u32[]{:S(2)}, u32[]{:S(2)}) %all-to-all-start) | async-done | bytes 2621472 | tf_op jit(solution)/shard_map/all_to_all | solution.py:75
  113.1 4.4 %copy.54 = bf16[1,5,8,256,128]{4,3,1,2,0:T(8,128)(2,1)} copy(bf16[1,5,8,256,128]{4,1,3,2,0:T(8,128)(2,1)} %bitcast.1) | data formatting | bytes 5242880 | tf_op jit(solution)/shard_map/all_to_all | solution.py:75
  117.6 5.3 %gather_fusion = bf16[16,5,256,128]{3,2,1,0:T(8,128)(2,1)} fusion(bf16[8,5,256,128]{3,2,1,0:T(8,128)(2,1)} %bitcast.95, s32[1024]{0:T(1024)S(1)} %pad_clamp_fusion.1), kind=kCustom, calls=%fused_computation.2 | custom fusion | bytes 10485824 | tf_op jit(solution)/shard_map/jit(_take)/gather | solution.py:78
  122.9 5.5 %select_select_fusion = bf16[16,5,256,128]{3,2,1,0:T(8,128)(2,1)} fusion(bf16[16,5,256,128]{3,2,1,0:T(8,128)(2,1)} %gather_fusion, pred[16]{0:T(512)(128)(4,1)S(1)} %get-tuple-element.41, pred[16]{0:T(512)(128)(4,1)S(1)} %get-tuple-element.65), kind=kLoop, calls=%fused_computation.27 | loop fusion | flops 5242880 | bytes 10485792 | tf_op jit(solution)/shard_map/jit(_where)/select_n | solution.py:80
  128.3 4.6 %all-to-all-start.1 = ((bf16[16,5,256,128]{3,2,1,0:T(8,128)(2,1)}), bf16[16,5,256,128]{3,2,1,0:T(8,128)(2,1)}, u32[]{:S(2)}, u32[]{:S(2)}) async-start(bf16[16,5,256,128]{3,2,1,0:T(8,128)(2,1)} %select_select_fusion), calls=%async_computation.1 | async-start | bytes 10485760 | tf_op jit(solution)/shard_map/all_to_all | solution.py:79
  133.2 4.6 %copy.44 = bf16[2048,640]{0,1:T(8,128)(2,1)} copy(bf16[2048,640]{1,0:T(8,128)(2,1)} %param.16) | data formatting | bytes 5242880 | tf_op args[3]
  137.8 0.5 multiply_reduce_fusion
  138.3 3.4 fusion.45
  141.7 1.0 copy-done.4
  142.8 0.8 slice.176
  143.6 1.2 multiply_reduce_fusion.2
  144.9 2.4 multiply_reduce_fusion.1
  148.7 0.6 fusion.89
  149.3 1.3 iota_compare_fusion.2
  150.7 0.6 fusion.17
  151.3 96.6 %all-to-all-done.1 = bf16[16,5,256,128]{3,2,1,0:T(8,128)(2,1)} async-done(((bf16[16,5,256,128]{3,2,1,0:T(8,128)(2,1)}), bf16[16,5,256,128]{3,2,1,0:T(8,128)(2,1)}, u32[]{:S(2)}, u32[]{:S(2)}) %all-to-all-start.1) | async-done | bytes 5242912 | tf_op jit(solution)/shard_map/all_to_all | solution.py:79
  247.9 2.8 copy.43
  250.7 1.2 bitcast_select_fusion
  252.0 4.1 %fusion.14 = (bf16[5,2304,128]{2,1,0:T(8,128)(2,1)}, bf16[5,2304,128]{2,1,0:T(8,128)(2,1)}) fusion(bf16[2,5,2048,128]{3,2,1,0:T(8,128)(2,1)S(1)} %bitcast_select_fusion, bf16[2,5,256,128]{3,2,1,0:T(8,128)(2,1)S(1)} %copy.45), kind=kLoop, calls=%fused_computation.33 | loop fusion | flops 11796480 | bytes 11796480 | tf_op jit(solution)/shard_map/squeeze | solution.py:119
  256.1 4.6 %gather_fusion.1 = bf16[5,2304,128]{2,1,0:T(8,128)(2,1)} fusion(bf16[5,2304,128]{2,1,0:T(8,128)(2,1)} %get-tuple-element.49, s32[1024]{0:T(1024)S(1)} %pad_clamp_fusion), kind=kCustom, calls=%fused_computation.clone | custom fusion | bytes 5898260 | tf_op jit(solution)/shard_map/jit(_take)/gather | solution.py:119
  260.7 5.4 %copy.46 = bf16[5,2304,128]{1,2,0:T(8,128)(2,1)} copy(bf16[5,2304,128]{2,1,0:T(8,128)(2,1)} %gather_fusion.1) | data formatting | bytes 5898240 | tf_op jit(solution)/shard_map/jit(_take)/gather | solution.py:119
  266.1 4.6 %gather_fusion.2 = bf16[5,2304,128]{2,1,0:T(8,128)(2,1)} fusion(bf16[5,2304,128]{2,1,0:T(8,128)(2,1)} %get-tuple-element.50, s32[1024]{0:T(1024)S(1)} %pad_clamp_fusion), kind=kCustom, calls=%fused_computation.1.clone | custom fusion | bytes 5898260 | tf_op jit(solution)/shard_map/jit(_take)/gather | solution.py:119
  270.8 5.4 %copy.47 = bf16[5,2304,128]{1,2,0:T(8,128)(2,1)} copy(bf16[5,2304,128]{2,1,0:T(8,128)(2,1)} %gather_fusion.2) | data formatting | bytes 5898240 | tf_op jit(solution)/shard_map/jit(_take)/gather | solution.py:119
  276.2 5.8 %broadcast_select_fusion.1 = (bf16[5,2304,128]{1,2,0:T(8,128)(2,1)}, bf16[5,2304,128]{1,2,0:T(8,128)(2,1)}) fusion(bf16[5,2304,128]{1,2,0:T(8,128)(2,1)} %copy.46, pred[5]{0:T(512)(128)(4,1)S(1)} %compare_and_fusion, bf16[5,2304,128]{1,2,0:T(8,128)(2,1)} %copy.47), kind=kLoop, calls=%fused_computation.37 | loop fusion | flops 2949120 | bytes 11796485 | tf_op jit(solution)/shard_map/jit(_take)/select_n | solution.py:119
  282.0 5.2 %fusion.90 = f32[5,256]{1,0:T(8,128)S(1)} fusion(pred[256,2304]{1,0:T(8,128)(4,1)S(1)} %get-tuple-element.58, bf16[5,2304,128]{1,2,0:T(8,128)(2,1)} %get-tuple-element.62, bf16[2,256,5,32]{1,3,2,0:T(8,128)(2,1)S(1)} %get-tuple-element.52, bf16[2,256,5,32]{1,3,2,0:T(8,128)(2,1)S(1)} %get-tuple-element.51), kind=kOutput, calls=%fused_computation.119 | convolution fusion | flops 389613824 | bytes 2397184 | tf_op jit(solution)/shard_map/sub | solution.py:43
  287.2 7.0 %fusion.37 = bf16[5,64,256]{2,1,0:T(8,128)(2,1)} fusion(f32[5,256]{1,0:T(8,128)S(1)} %fusion.90, bf16[5,2304,128]{1,2,0:T(8,128)(2,1)} %get-tuple-element.62, pred[256,2304]{1,0:T(8,128)(4,1)S(1)} %get-tuple-element.58, bf16[2,256,5,32]{1,3,2,0:T(8,128)(2,1)S(1)} %get-tuple-element.52, bf16[2,256,5,32]{1,3,2,0:T(8,128)(2,1)S(1)} %get-tuple-element.51), kind=kOutput, calls=%fused_computation.54 | convolution fusion | flops 770133504 | bytes 4035584 | tf_op jit(solution)/shard_map/hqk,hkd->qhd/dot_general | solution.py:45
  294.2 5.5 %fusion.95 = f32[5,256]{1,0:T(8,128)S(1)} fusion(pred[256,2304]{1,0:T(8,128)(4,1)S(1)} %get-tuple-element.57, bf16[5,2304,128]{1,2,0:T(8,128)(2,1)} %get-tuple-element.61, bf16[2,256,5,32]{1,3,2,0:T(8,128)(2,1)S(1)} %get-tuple-element.51, bf16[2,256,5,32]{1,3,2,0:T(8,128)(2,1)S(1)} %get-tuple-element.52), kind=kOutput, calls=%fused_computation.120 | convolution fusion | flops 389613824 | bytes 2397184 | tf_op jit(solution)/shard_map/sub | solution.py:43
  299.6 6.3 %fusion.40 = bf16[5,64,256]{2,1,0:T(8,128)(2,1)S(1)} fusion(f32[5,256]{1,0:T(8,128)S(1)} %fusion.95, bf16[5,2304,128]{1,2,0:T(8,128)(2,1)} %get-tuple-element.61, pred[256,2304]{1,0:T(8,128)(4,1)S(1)} %get-tuple-element.57, bf16[2,256,5,32]{1,3,2,0:T(8,128)(2,1)S(1)} %get-tuple-element.51, bf16[2,256,5,32]{1,3,2,0:T(8,128)(2,1)S(1)} %get-tuple-element.52), kind=kOutput, calls=%fused_computation.55 | convolution fusion | flops 770133504 | bytes 4035584 | tf_op jit(solution)/shard_map/hqk,hkd->qhd/dot_general | solution.py:45
  306.0 3.3 fusion.47
  309.3 0.6 copy-done.14
  310.1 5.6 %concatenate.30 = bf16[2,5,2304,128]{3,2,1,0:T(8,128)(2,1)} pad(bf16[2,5,2048,128]{3,2,1,0:T(8,128)(2,1)} %copy-done.1, bf16[]{:T(256)} %constant.52.clone.1), padding=0_0x0_0x0_256x0_0 | pad | bytes 11141122 | tf_op jit(solution)/shard_map/concatenate | solution.py:131
  315.7 24.9 %while.1 = (s32[]{:T(128)}, bf16[2,5,2304,128]{3,2,1,0:T(8,128)(2,1)}, s32[2,4]{1,0:T(2,128)S(1)}, bf16[2,5,256,128]{3,2,1,0:T(8,128)(2,1)S(1)}, s32[]{:T(128)}, /*index=5*/s32[4]{0:T(128)S(1)}, s32[]{:T(128)}) while((s32[]{:T(128)}, bf16[2,5,2304,128]{3,2,1,0:T(8,128)(2,1)}, s32[2,4]{1,0:T(2,128)S(1)}, bf16[2,5,256,128]{3,2,1,0:T(8,128)(2,1)S(1)}, ...), condition=%wide.while_cond, body=%wide.while_body.sunk | while | flops 163869 | bytes 1638603 | solution.py:136
  315.7 0.6 fusion.104
  316.3 3.2 and_reduce_fusion.2
  319.5 3.0 dynamic-slice_select_fusion.2
  322.5 5.6 %dynamic-update-slice.3 = bf16[2,5,2304,128]{3,2,1,0:T(8,128)(2,1)} dynamic-update-slice(bf16[2,5,2304,128]{3,2,1,0:T(8,128)(2,1)} %get-tuple-element.113, bf16[1,5,256,128]{3,2,1,0:T(8,128)(2,1)S(1)} %dynamic-slice_select_fusion.2, s32[]{:T(128)} %bitcast.89, s32[]{:T(128)} %constant.38.clone.1..sunk, s32[]{:T(128)} %bitcast.90, s32[]{:T(128)} %constant.38.clone.1..sunk) | dynamic-update-slice | bytes 655364 | tf_op jit(solution)/shard_map/vmap(vmap())/scatter
  328.1 0.6 fusion.104
  328.7 3.2 and_reduce_fusion.2
  332.0 3.0 dynamic-slice_select_fusion.2
  335.0 5.6 %dynamic-update-slice.3 = bf16[2,5,2304,128]{3,2,1,0:T(8,128)(2,1)} dynamic-update-slice(bf16[2,5,2304,128]{3,2,1,0:T(8,128)(2,1)} %get-tuple-element.113, bf16[1,5,256,128]{3,2,1,0:T(8,128)(2,1)S(1)} %dynamic-slice_select_fusion.2, s32[]{:T(128)} %bitcast.89, s32[]{:T(128)} %constant.38.clone.1..sunk, s32[]{:T(128)} %bitcast.90, s32[]{:T(128)} %constant.38.clone.1..sunk) | dynamic-update-slice | bytes 655364 | tf_op jit(solution)/shard_map/vmap(vmap())/scatter
  340.5 2.7 constant_dynamic-slice_fusion.2
  343.3 1.7 collective-permute-start
  344.9 15.9 %collective-permute-done = bf16[2,5,288,128]{3,2,1,0:T(8,128)(2,1)} collective-permute-done((bf16[2,5,288,128]{3,2,1,0:T(8,128)(2,1)}, bf16[2,5,288,128]{3,2,1,0:T(8,128)(2,1)}, u32[]{:S(2)}, u32[]{:S(2)}) %collective-permute-start) | collective-permute-done | bytes 737312 | tf_op jit(solution)/shard_map/ppermute | solution.py:11
  360.8 3.2 maximum_select_fusion
  364.0 30.0 %all-reduce.3.cloned.1.call-done = f32[512,2048]{1,0:T(8,128)} async-done(((f32[512,2048]{1,0:T(8,128)}), f32[512,2048]{1,0:T(8,128)}) %all-reduce.3.cloned.1.call-update) | async-done | bytes 4194320 | tf_op jit(solution)/shard_map/psum | solution.py:128
  394.0 4.2 %fusion.12 = bf16[512,2048]{1,0:T(8,128)(2,1)} fusion(f32[512,2048]{1,0:T(8,128)} %all-reduce.3.cloned.1.call-done, bf16[2,256,2048]{2,1,0:T(8,128)(2,1)S(1)} %copy-done.3), kind=kLoop, calls=%fused_computation.29 | loop fusion | flops 3145728 | bytes 8388608 | tf_op jit(solution)/shard_map/convert_element_type | solution.py:129
  (58 shorter events, 2.1 us)
Async XLA Ops:
  7.2 298.8 %copy-start = (bf16[320,2048]{1,0:T(8,128)(2,1)S(1)}, bf16[320,2048]{1,0:T(8,128)(2,1)}, u32[]{:S(2)}) copy-start(bf16[320,2048]{1,0:T(8,128)(2,1)} %param.17) | copy-start | bytes 3932164
  12.4 7.4 %copy-start.9 = (s32[16]{0:T(128)S(1)}, s32[16]{0:T(128)}, u32[]{:S(2)}) copy-start(s32[16]{0:T(128)} %param.21) | copy-start | bytes 196
  12.4 7.4 %copy-start.12 = (s32[16]{0:T(128)S(1)}, s32[16]{0:T(128)}, u32[]{:S(2)}) copy-start(s32[16]{0:T(128)} %param.22) | copy-start | bytes 196
  12.4 100.7 %all-to-all-start = ((bf16[1,5,2048,128]{3,1,0,2:T(8,128)(2,1)}), bf16[1,5,2048,128]{3,1,0,2:T(8,128)(2,1)}, u32[]{:S(2)}, u32[]{:S(2)}) async-start(bf16[1,5,2048,128]{3,1,0,2:T(8,128)(2,1)} %copy.40), calls=%async_computation | async-start | bytes 8388608 | tf_op jit(solution)/shard_map/all_to_all | solution.py:75
  128.3 119.6 %all-to-all-start.1 = ((bf16[16,5,256,128]{3,2,1,0:T(8,128)(2,1)}), bf16[16,5,256,128]{3,2,1,0:T(8,128)(2,1)}, u32[]{:S(2)}, u32[]{:S(2)}) async-start(bf16[16,5,256,128]{3,2,1,0:T(8,128)(2,1)} %select_select_fusion), calls=%async_computation.1 | async-start | bytes 10485760 | tf_op jit(solution)/shard_map/all_to_all | solution.py:79
  133.0 4.8 %copy-start.2 = (bf16[2,256,2048]{2,1,0:T(8,128)(2,1)S(1)}, bf16[2,256,2048]{2,1,0:T(8,128)(2,1)}, u32[]{:S(2)}) copy-start(bf16[2,256,2048]{2,1,0:T(8,128)(2,1)} %param.13) | copy-start | bytes 6291460
  133.0 261.0 %all-reduce.3.cloned.1.call-start = ((), (), s32[]{:S(2)}) async-start(), calls=%async_computation.2 | async-start | bytes 8388608 | tf_op jit(solution)/shard_map/psum | solution.py:128
  133.2 5.1 %copy-start.15 = (f32[2048]{0:T(1024)S(1)}, f32[2048]{0:T(1024)}, u32[]{:S(2)}) copy-start(f32[2048]{0:T(1024)} %param.14) | copy-start | bytes 24580
  138.3 5.2 %copy-start.13 = (s32[16]{0:T(128)S(1)}, s32[16]{0:T(128)}, u32[]{:S(2)}) copy-start(s32[16]{0:T(128)} %param.23) | copy-start | bytes 196
  141.7 1.1 copy-start.4
  144.9 2.8 copy-start.5
  144.9 2.8 copy-start.10
  144.9 2.8 copy-start.11
  147.3 1.0 copy-start.6
  252.0 4.1 %copy-start.1 = (bf16[2,5,2048,128]{3,2,1,0:T(8,128)(2,1)}, bf16[2,5,2048,128]{3,2,1,0:T(8,128)(2,1)S(1)}, u32[]{:S(2)}) copy-start(bf16[2,5,2048,128]{3,2,1,0:T(8,128)(2,1)S(1)} %bitcast_select_fusion) | copy-start | bytes 15728644
  299.6 6.4 %copy-start.7 = (bf16[5,64,256]{2,1,0:T(8,128)(2,1)S(1)}, bf16[5,64,256]{2,1,0:T(8,128)(2,1)}, u32[]{:S(2)}) copy-start(bf16[5,64,256]{2,1,0:T(8,128)(2,1)} %fusion.37) | copy-start | bytes 491524
  309.3 0.7 copy-start.14
  310.1 5.6 %copy-start.8 = (s32[4]{0:T(128)S(1)}, s32[4]{0:T(128)}, u32[]{:S(2)}) copy-start(s32[4]{0:T(128)} %constant.238) | copy-start | bytes 52
  340.5 53.4 %copy-start.3 = (bf16[2,256,2048]{2,1,0:T(8,128)(2,1)S(1)}, bf16[2,256,2048]{2,1,0:T(8,128)(2,1)}, u32[]{:S(2)}) copy-start(bf16[2,256,2048]{2,1,0:T(8,128)(2,1)} %param.13) | copy-start | bytes 6291460
  343.3 17.6 %collective-permute-start = (bf16[2,5,288,128]{3,2,1,0:T(8,128)(2,1)}, bf16[2,5,288,128]{3,2,1,0:T(8,128)(2,1)}, u32[]{:S(2)}, u32[]{:S(2)}) collective-permute-start(bf16[2,5,288,128]{3,2,1,0:T(8,128)(2,1)} %get-tuple-element.48), channel_id=1, source_target_pairs={{0,4},{4,0},{8,12},{12,8},{16,20},{20,16},{24,28},{28,24},{1,5},{5... | collective-permute-start | bytes 2211848 | tf_op jit(solution)/shard_map/ppermute | solution.py:11
Sparse Core Ops, SparseCore 0:
  309.4 84.5 all-reduce.2
where the time goes:
time: 407 us; the launch traced here: 405 us
  waiting for transfers between devices  236 us (58%)
  local copies, waits for them, and re-layouts  66.8 us (16%)
  other arithmetic  41.1 us (10%)
  matrix products  33 us (8%)
  between operations  14.3 us (4%)
  starting transfers between devices  13.9 us (3%)
    all_to_all x1, waiting for transfers between devices, on_device(): lax.all_to_all(jnp.where(live_all[:, None, None, None], select_chosen, jn...  96.6 us
    all_to_all x1, waiting for transfers between devices, on_device(): lax.all_to_all(stored, 'req', split_axis=2, concat_axis=0, tiled=True)  93.2 us
    psum x1, waiting for transfers between devices, on_device(): lax.psum(jnp.dot(mixed_all, w_out, preferred_element_type=jnp.float32), '...  30 us
    gather x4, local copies, waits for them, and re-layouts, on_device(): chosen = jnp.take(keys_all[number], head_select, axis=0)  20.1 us
    ppermute x1, waiting for transfers between devices, swapped(): return lax.ppermute(value, axis, pairs)  15.9 us
    dot_general x2, matrix products, attend(): jnp.einsum('hqk,hkd->qhd', probs, keys_one[..., head_dim:], preferred_ele...  13.3 us
    scatter x6, local copies, waits for them, and re-layouts  12.4 us
    scatter x4, other arithmetic  12.4 us
  transfers between devices with their start and end apart: 4, of which 4 were waited for; matrix products, arithmetic and copies ran while one was open for 13% of the time, Pallas kernels for 0%

commit v1 on v0

--- a/solution.py
+++ b/solution.py
@@ -125,7 +125,9 @@
         mixed = attend(query_one, chosen, allowed, head_dim, new_count, scale)
         outputs.append(mixed)
     mixed_all = jnp.concatenate(outputs, axis=0)
-    summed = lax.psum(jnp.dot(mixed_all, w_out, preferred_element_type=jnp.float32), "tp")
+    summed = jnp.sum(
+        lax.all_gather(jnp.dot(mixed_all, w_out, preferred_element_type=jnp.float32), "tp"), axis=0
+    )
     layer = (token_rows.astype(jnp.float32) + summed).astype(jnp.bfloat16)
     layer = layer.reshape(req_dev, new_count, width)
     padded_tokens = jnp.concatenate(

time: 407 us -> 438 us (1.076)
  waiting for transfers between devices: 236 us -> 259 us
  other arithmetic: 41.1 us -> 49.8 us
    all_gather x0 -> x1, waiting for transfers between devices: none -> 53.6 us  [on_device(): lax.all_gather(jnp.dot(mixed_all, w_out, preferred_element_type=jnp.float...]
    psum x1 -> x0, waiting for transfers between devices: 30 us -> none  [on_device(): lax.psum(jnp.dot(mixed_all, w_out, preferred_element_type=jnp.float32), '...]
    reduce_sum x0 -> x1, other arithmetic: none -> 10.2 us  [on_device(): jnp.sum(lax.all_gather(jnp.dot(mixed_all, w_out, preferred_element_type=j...]
  transfers between devices with their start and end apart: 4 -> 4, of which waited for: 4 -> 4; matrix products, arithmetic and copies ran while one was open for 13% -> 12% of each run, Pallas kernels for 0% -> 0%
where the time goes in v1:
time: 438 us; the launch traced here: 436 us
  waiting for transfers between devices  259 us (59%)
  local copies, waits for them, and re-layouts  65.9 us (15%)
  other arithmetic  49.8 us (11%)
  matrix products  33.1 us (8%)
  between operations  14.4 us (3%)
  starting transfers between devices  13.6 us (3%)
    all_to_all x1, waiting for transfers between devices, on_device(): lax.all_to_all(jnp.where(live_all[:, None, None, None], select_chosen, jn...  96.6 us
    all_to_all x1, waiting for transfers between devices, on_device(): lax.all_to_all(stored, 'req', split_axis=2, concat_axis=0, tiled=True)  93.2 us
    all_gather x1, waiting for transfers between devices, on_device(): lax.all_gather(jnp.dot(mixed_all, w_out, preferred_element_type=jnp.float...  53.6 us
    gather x4, local copies, waits for them, and re-layouts, on_device(): chosen = jnp.take(keys_all[number], head_select, axis=0)  20 us
    ppermute x1, waiting for transfers between devices, swapped(): return lax.ppermute(value, axis, pairs)  15.6 us
    dot_general x2, matrix products, attend(): jnp.einsum('hqk,hkd->qhd', probs, keys_one[..., head_dim:], preferred_ele...  13.3 us
    scatter x6, local copies, waits for them, and re-layouts  12.5 us
    scatter x4, other arithmetic  12.5 us
  transfers between devices with their start and end apart: 4, of which 4 were waited for; matrix products, arithmetic and copies ran while one was open for 12% of the time, Pallas kernels for 0%

profile of v1, /device:TPU:0, one launch (start us, length us, event | category | flops | bytes accessed | tf_op | source)
XLA Modules:
  0.0 435.9 jit_solution(16942815588735358366)
XLA Ops:
  7.2 5.2 %copy.40 = bf16[1,5,2048,128]{3,1,0,2:T(8,128)(2,1)} copy(bf16[1,5,2048,128]{3,2,1,0:T(8,128)(2,1)} %param.20) | data formatting | bytes 5242880 | tf_op args[7]
  12.4 7.4 %all-to-all-start = ((bf16[1,5,2048,128]{3,1,0,2:T(8,128)(2,1)}), bf16[1,5,2048,128]{3,1,0,2:T(8,128)(2,1)}, u32[]{:S(2)}, u32[]{:S(2)}) async-start(bf16[1,5,2048,128]{3,1,0,2:T(8,128)(2,1)} %copy.40), calls=%async_computation | async-start | bytes 8388608 | tf_op jit(solution)/shard_map/all_to_all | solution.py:75
  19.9 93.2 %all-to-all-done = bf16[1,5,2048,128]{3,1,0,2:T(8,128)(2,1)} async-done(((bf16[1,5,2048,128]{3,1,0,2:T(8,128)(2,1)}), bf16[1,5,2048,128]{3,1,0,2:T(8,128)(2,1)}, u32[]{:S(2)}, u32[]{:S(2)}) %all-to-all-start) | async-done | bytes 2621472 | tf_op jit(solution)/shard_map/all_to_all | solution.py:75
  113.1 4.4 %copy.54 = bf16[1,5,8,256,128]{4,3,1,2,0:T(8,128)(2,1)} copy(bf16[1,5,8,256,128]{4,1,3,2,0:T(8,128)(2,1)} %bitcast) | data formatting | bytes 5242880 | tf_op jit(solution)/shard_map/all_to_all | solution.py:75
  117.6 5.3 %gather_fusion = bf16[16,5,256,128]{3,2,1,0:T(8,128)(2,1)} fusion(bf16[8,5,256,128]{3,2,1,0:T(8,128)(2,1)} %bitcast.92, s32[1024]{0:T(1024)S(1)} %pad_clamp_fusion.1), kind=kCustom, calls=%fused_computation.2 | custom fusion | bytes 10485824 | tf_op jit(solution)/shard_map/jit(_take)/gather | solution.py:78
  122.9 5.5 %select_select_fusion = bf16[16,5,256,128]{3,2,1,0:T(8,128)(2,1)} fusion(bf16[16,5,256,128]{3,2,1,0:T(8,128)(2,1)} %gather_fusion, pred[16]{0:T(512)(128)(4,1)S(1)} %get-tuple-element.41, pred[16]{0:T(512)(128)(4,1)S(1)} %get-tuple-element.65), kind=kLoop, calls=%fused_computation.30 | loop fusion | flops 5242880 | bytes 10485792 | tf_op jit(solution)/shard_map/jit(_where)/select_n | solution.py:80
  128.3 4.6 %all-to-all-start.1 = ((bf16[16,5,256,128]{3,2,1,0:T(8,128)(2,1)}), bf16[16,5,256,128]{3,2,1,0:T(8,128)(2,1)}, u32[]{:S(2)}, u32[]{:S(2)}) async-start(bf16[16,5,256,128]{3,2,1,0:T(8,128)(2,1)} %select_select_fusion), calls=%async_computation.1 | async-start | bytes 10485760 | tf_op jit(solution)/shard_map/all_to_all | solution.py:79
  133.2 4.6 %copy.44 = bf16[2048,640]{0,1:T(8,128)(2,1)} copy(bf16[2048,640]{1,0:T(8,128)(2,1)} %param.16) | data formatting | bytes 5242880 | tf_op args[3]
  138.3 3.4 fusion.48
  141.7 1.0 copy-done.4
  142.8 0.8 slice.176
  143.6 1.2 multiply_reduce_fusion.1
  144.9 2.4 multiply_reduce_fusion
  148.7 0.6 fusion.92
  149.3 1.3 iota_compare_fusion.2
  150.7 0.6 fusion.20
  151.3 96.6 %all-to-all-done.1 = bf16[16,5,256,128]{3,2,1,0:T(8,128)(2,1)} async-done(((bf16[16,5,256,128]{3,2,1,0:T(8,128)(2,1)}), bf16[16,5,256,128]{3,2,1,0:T(8,128)(2,1)}, u32[]{:S(2)}, u32[]{:S(2)}) %all-to-all-start.1) | async-done | bytes 5242912 | tf_op jit(solution)/shard_map/all_to_all | solution.py:79
  247.9 2.8 copy.43
  250.7 1.2 bitcast_select_fusion
  252.0 4.3 fusion.17
  256.2 4.5 %gather_fusion.1 = bf16[5,2304,128]{2,1,0:T(8,128)(2,1)} fusion(bf16[5,2304,128]{2,1,0:T(8,128)(2,1)} %get-tuple-element.49, s32[1024]{0:T(1024)S(1)} %pad_clamp_fusion), kind=kCustom, calls=%fused_computation.clone | custom fusion | bytes 5898260 | tf_op jit(solution)/shard_map/jit(_take)/gather | solution.py:119
  260.8 4.6 %gather_fusion.2 = bf16[5,2304,128]{2,1,0:T(8,128)(2,1)} fusion(bf16[5,2304,128]{2,1,0:T(8,128)(2,1)} %get-tuple-element.50, s32[1024]{0:T(1024)S(1)} %pad_clamp_fusion), kind=kCustom, calls=%fused_computation.1.clone | custom fusion | bytes 5898260 | tf_op jit(solution)/shard_map/jit(_take)/gather | solution.py:119
  265.4 5.4 %copy.47 = bf16[5,2304,128]{1,2,0:T(8,128)(2,1)} copy(bf16[5,2304,128]{2,1,0:T(8,128)(2,1)} %gather_fusion.2) | data formatting | bytes 5898240 | tf_op jit(solution)/shard_map/jit(_take)/gather | solution.py:119
  270.8 5.5 %copy.46 = bf16[5,2304,128]{1,2,0:T(8,128)(2,1)} copy(bf16[5,2304,128]{2,1,0:T(8,128)(2,1)} %gather_fusion.1) | data formatting | bytes 5898240 | tf_op jit(solution)/shard_map/jit(_take)/gather | solution.py:119
  276.2 5.9 %broadcast_select_fusion.1 = (bf16[5,2304,128]{1,2,0:T(8,128)(2,1)}, bf16[5,2304,128]{1,2,0:T(8,128)(2,1)}) fusion(bf16[5,2304,128]{1,2,0:T(8,128)(2,1)} %copy.46, pred[5]{0:T(512)(128)(4,1)S(1)} %compare_and_fusion, bf16[5,2304,128]{1,2,0:T(8,128)(2,1)} %copy.47), kind=kLoop, calls=%fused_computation.40 | loop fusion | flops 2949120 | bytes 11796485 | tf_op jit(solution)/shard_map/jit(_take)/select_n | solution.py:119
  282.1 5.2 %fusion.98 = f32[5,256]{1,0:T(8,128)S(1)} fusion(pred[256,2304]{1,0:T(8,128)(4,1)S(1)} %get-tuple-element.57, bf16[5,2304,128]{1,2,0:T(8,128)(2,1)} %get-tuple-element.61, bf16[2,256,5,32]{1,3,2,0:T(8,128)(2,1)S(1)} %get-tuple-element.51, bf16[2,256,5,32]{1,3,2,0:T(8,128)(2,1)S(1)} %get-tuple-element.52), kind=kOutput, calls=%fused_computation.123 | convolution fusion | flops 389613824 | bytes 2397184 | tf_op jit(solution)/shard_map/sub | solution.py:43
  287.3 7.0 %fusion.43 = bf16[5,64,256]{2,1,0:T(8,128)(2,1)} fusion(f32[5,256]{1,0:T(8,128)S(1)} %fusion.98, bf16[5,2304,128]{1,2,0:T(8,128)(2,1)} %get-tuple-element.61, pred[256,2304]{1,0:T(8,128)(4,1)S(1)} %get-tuple-element.57, bf16[2,256,5,32]{1,3,2,0:T(8,128)(2,1)S(1)} %get-tuple-element.51, bf16[2,256,5,32]{1,3,2,0:T(8,128)(2,1)S(1)} %get-tuple-element.52), kind=kOutput, calls=%fused_computation.58 | convolution fusion | flops 770133504 | bytes 4035584 | tf_op jit(solution)/shard_map/hqk,hkd->qhd/dot_general | solution.py:45
  294.3 5.5 %fusion.93 = f32[5,256]{1,0:T(8,128)S(1)} fusion(pred[256,2304]{1,0:T(8,128)(4,1)S(1)} %get-tuple-element.58, bf16[5,2304,128]{1,2,0:T(8,128)(2,1)} %get-tuple-element.62, bf16[2,256,5,32]{1,3,2,0:T(8,128)(2,1)S(1)} %get-tuple-element.52, bf16[2,256,5,32]{1,3,2,0:T(8,128)(2,1)S(1)} %get-tuple-element.51), kind=kOutput, calls=%fused_computation.122 | convolution fusion | flops 389613824 | bytes 2397184 | tf_op jit(solution)/shard_map/sub | solution.py:43
  299.8 6.3 %fusion.40 = bf16[5,64,256]{2,1,0:T(8,128)(2,1)S(1)} fusion(f32[5,256]{1,0:T(8,128)S(1)} %fusion.93, bf16[5,2304,128]{1,2,0:T(8,128)(2,1)} %get-tuple-element.62, pred[256,2304]{1,0:T(8,128)(4,1)S(1)} %get-tuple-element.58, bf16[2,256,5,32]{1,3,2,0:T(8,128)(2,1)S(1)} %get-tuple-element.52, bf16[2,256,5,32]{1,3,2,0:T(8,128)(2,1)S(1)} %get-tuple-element.51), kind=kOutput, calls=%fused_computation.57 | convolution fusion | flops 770133504 | bytes 4035584 | tf_op jit(solution)/shard_map/hqk,hkd->qhd/dot_general | solution.py:45
  306.1 3.3 fusion.50
  309.5 0.6 copy-done.14
  310.3 5.9 %concatenate.30 = bf16[2,5,2304,128]{3,2,1,0:T(8,128)(2,1)} pad(bf16[2,5,2048,128]{3,2,1,0:T(8,128)(2,1)} %copy-done.1, bf16[]{:T(256)} %constant.52.clone.1), padding=0_0x0_0x0_256x0_0 | pad | bytes 11141122 | tf_op jit(solution)/shard_map/concatenate | solution.py:133
  316.3 25.0 %while.1 = (s32[]{:T(128)}, bf16[2,5,2304,128]{3,2,1,0:T(8,128)(2,1)}, s32[2,4]{1,0:T(2,128)S(1)}, bf16[2,5,256,128]{3,2,1,0:T(8,128)(2,1)S(1)}, s32[]{:T(128)}, /*index=5*/s32[4]{0:T(128)S(1)}, s32[]{:T(128)}) while((s32[]{:T(128)}, bf16[2,5,2304,128]{3,2,1,0:T(8,128)(2,1)}, s32[2,4]{1,0:T(2,128)S(1)}, bf16[2,5,256,128]{3,2,1,0:T(8,128)(2,1)S(1)}, ...), condition=%wide.while_cond, body=%wide.while_body.sunk | while | flops 163869 | bytes 1638603 | solution.py:138
  316.3 0.6 fusion.107
  316.9 3.3 and_reduce_fusion.2
  320.1 3.0 dynamic-slice_select_fusion.2
  323.1 5.7 %dynamic-update-slice.3 = bf16[2,5,2304,128]{3,2,1,0:T(8,128)(2,1)} dynamic-update-slice(bf16[2,5,2304,128]{3,2,1,0:T(8,128)(2,1)} %get-tuple-element.113, bf16[1,5,256,128]{3,2,1,0:T(8,128)(2,1)S(1)} %dynamic-slice_select_fusion.2, s32[]{:T(128)} %bitcast.86, s32[]{:T(128)} %constant.38.clone.1..sunk, s32[]{:T(128)} %bitcast.87, s32[]{:T(128)} %constant.38.clone.1..sunk) | dynamic-update-slice | bytes 655364 | tf_op jit(solution)/shard_map/vmap(vmap())/scatter
  328.8 0.6 fusion.107
  329.4 3.2 and_reduce_fusion.2
  332.7 3.0 dynamic-slice_select_fusion.2
  335.7 5.6 %dynamic-update-slice.3 = bf16[2,5,2304,128]{3,2,1,0:T(8,128)(2,1)} dynamic-update-slice(bf16[2,5,2304,128]{3,2,1,0:T(8,128)(2,1)} %get-tuple-element.113, bf16[1,5,256,128]{3,2,1,0:T(8,128)(2,1)S(1)} %dynamic-slice_select_fusion.2, s32[]{:T(128)} %bitcast.86, s32[]{:T(128)} %constant.38.clone.1..sunk, s32[]{:T(128)} %bitcast.87, s32[]{:T(128)} %constant.38.clone.1..sunk) | dynamic-update-slice | bytes 655364 | tf_op jit(solution)/shard_map/vmap(vmap())/scatter
  341.3 1.4 constant_dynamic-slice_fusion.2
  342.7 1.3 collective-permute-start
  344.1 15.6 %collective-permute-done = bf16[2,5,288,128]{3,2,1,0:T(8,128)(2,1)S(1)} collective-permute-done((bf16[2,5,288,128]{3,2,1,0:T(8,128)(2,1)S(1)}, bf16[2,5,288,128]{3,2,1,0:T(8,128)(2,1)S(1)}, u32[]{:S(2)}, u32[]{:S(2)}) %collective-permute-start) | collective-permute-done | bytes 737312 | tf_op jit(solution)/shard_map/ppermute | solution.py:11
  359.7 1.3 maximum_select_fusion
  361.0 53.6 %all-gather.3.cloned.1.call-done = f32[2048,2048]{1,0:T(8,128)} async-done(((f32[512,2048]{1,0:T(8,128)}), f32[2048,2048]{1,0:T(8,128)}) %all-gather.3.cloned.1.call-update) | async-done | bytes 16777232 | tf_op jit(solution)/shard_map/all_gather | solution.py:129
  414.6 10.2 %reduce_sum.61 = f32[512,2048]{1,0:T(8,128)} reduce(f32[4,512,2048]{2,1,0:T(8,128)} %bitcast.93, f32[]{:T(128)} %constant.53.clone.1), dimensions={0}, to_apply=%region_7.9 | reduce | flops 3145728 | bytes 20971524 | tf_op jit(solution)/shard_map/reduce_sum | solution.py:128
  424.9 4.2 fusion.15
  (59 shorter events, 2.6 us)
Async XLA Ops:
  7.2 299.0 %copy-start = (bf16[320,2048]{1,0:T(8,128)(2,1)S(1)}, bf16[320,2048]{1,0:T(8,128)(2,1)}, u32[]{:S(2)}) copy-start(bf16[320,2048]{1,0:T(8,128)(2,1)} %param.17) | copy-start | bytes 3932164
  12.4 7.4 %copy-start.9 = (s32[16]{0:T(128)S(1)}, s32[16]{0:T(128)}, u32[]{:S(2)}) copy-start(s32[16]{0:T(128)} %param.21) | copy-start | bytes 196
  12.4 7.4 %copy-start.12 = (s32[16]{0:T(128)S(1)}, s32[16]{0:T(128)}, u32[]{:S(2)}) copy-start(s32[16]{0:T(128)} %param.22) | copy-start | bytes 196
  12.4 100.7 %all-to-all-start = ((bf16[1,5,2048,128]{3,1,0,2:T(8,128)(2,1)}), bf16[1,5,2048,128]{3,1,0,2:T(8,128)(2,1)}, u32[]{:S(2)}, u32[]{:S(2)}) async-start(bf16[1,5,2048,128]{3,1,0,2:T(8,128)(2,1)} %copy.40), calls=%async_computation | async-start | bytes 8388608 | tf_op jit(solution)/shard_map/all_to_all | solution.py:75
  128.3 119.6 %all-to-all-start.1 = ((bf16[16,5,256,128]{3,2,1,0:T(8,128)(2,1)}), bf16[16,5,256,128]{3,2,1,0:T(8,128)(2,1)}, u32[]{:S(2)}, u32[]{:S(2)}) async-start(bf16[16,5,256,128]{3,2,1,0:T(8,128)(2,1)} %select_select_fusion), calls=%async_computation.1 | async-start | bytes 10485760 | tf_op jit(solution)/shard_map/all_to_all | solution.py:79
  133.0 4.8 %copy-start.2 = (bf16[2,256,2048]{2,1,0:T(8,128)(2,1)S(1)}, bf16[2,256,2048]{2,1,0:T(8,128)(2,1)}, u32[]{:S(2)}) copy-start(bf16[2,256,2048]{2,1,0:T(8,128)(2,1)} %param.13) | copy-start | bytes 6291460
  133.0 281.6 %all-gather.3.cloned.1.call-start = ((), (), s32[]{:S(2)}) async-start(), calls=%async_computation.2 | async-start | bytes 20971520 | tf_op jit(solution)/shard_map/all_gather | solution.py:129
  133.2 5.1 %copy-start.15 = (f32[2048]{0:T(1024)S(1)}, f32[2048]{0:T(1024)}, u32[]{:S(2)}) copy-start(f32[2048]{0:T(1024)} %param.14) | copy-start | bytes 24580
  138.3 5.2 %copy-start.13 = (s32[16]{0:T(128)S(1)}, s32[16]{0:T(128)}, u32[]{:S(2)}) copy-start(s32[16]{0:T(128)} %param.23) | copy-start | bytes 196
  141.7 1.1 copy-start.4
  144.9 2.8 copy-start.5
  144.9 2.8 copy-start.10
  144.9 2.8 copy-start.11
  147.3 1.0 copy-start.6
  252.0 4.3 copy-start.1
  299.8 6.4 %copy-start.7 = (bf16[5,64,256]{2,1,0:T(8,128)(2,1)S(1)}, bf16[5,64,256]{2,1,0:T(8,128)(2,1)}, u32[]{:S(2)}) copy-start(bf16[5,64,256]{2,1,0:T(8,128)(2,1)} %fusion.43) | copy-start | bytes 491524
  309.5 0.7 copy-start.14
  310.3 5.9 %copy-start.8 = (s32[4]{0:T(128)S(1)}, s32[4]{0:T(128)}, u32[]{:S(2)}) copy-start(s32[4]{0:T(128)} %constant.241) | copy-start | bytes 52
  342.7 16.9 %collective-permute-start = (bf16[2,5,288,128]{3,2,1,0:T(8,128)(2,1)S(1)}, bf16[2,5,288,128]{3,2,1,0:T(8,128)(2,1)S(1)}, u32[]{:S(2)}, u32[]{:S(2)}) collective-permute-start(bf16[2,5,288,128]{3,2,1,0:T(8,128)(2,1)S(1)} %get-tuple-element.48), channel_id=1, source_target_pairs={{0,4},{4,0},{8,12},{12,8},{16,20},{20,16},{24,28},{28,24},{1,5},{5... | collective-permute-start | bytes 2211848 | tf_op jit(solution)/shard_map/ppermute | solution.py:11
  414.6 10.2 %copy-start.3 = (bf16[2,256,2048]{2,1,0:T(8,128)(2,1)S(1)}, bf16[2,256,2048]{2,1,0:T(8,128)(2,1)}, u32[]{:S(2)}) copy-start(bf16[2,256,2048]{2,1,0:T(8,128)(2,1)} %param.13) | copy-start | bytes 6291460
Sparse Core Ops, SparseCore 0:
  309.6 104.9 all-gather.2
